TPU v7x, 128 devices: a whole 4x4x4 slice. The times are simulated.
128 devices in a mesh: dp: 32 (over y, z, core), rep: 4 (over x).
Axes of the slice: x: 4, y: 4, z: 4, core: 2. Of those that a mesh axis runs over, the one named last changes fastest.
Arguments:
- queries: bfloat16 [8192, 768], P(('dp', 'rep')), may hold values from -60 to 60
- bank: bfloat16 [256, 4096, 768], P('dp', 'rep'), may hold values from -0.21875 to 0.21875
- labels: int32 [256, 4096], P('dp', 'rep'), may hold values from 0 to 127
- probes: int32 [8192, 8], P(('dp', 'rep')), may hold values from 0 to 255, all different within a row; in each aligned block of 64 rows (0 to 63, 64 to 127, ...) at most 4 rows name the same one
Outputs:
- votes: float32 [8192, 128], P(('dp', 'rep'))
Inputs may be any that keep to these rules, and one draw needn't show every extreme that they name: `probes`: each row names 8 different clusters; among the rows of one device no cluster is named more than 4 times.
All inputs are finite; a program needn't handle non-finite values.
Results may differ from a plain program's by a relative error of at most 0.0017.
Values may be sent and summed in bfloat16 or wider, within the bound.
No kernel may reach another device: no remote copies, remote signals or barrier semaphores. Data moves between devices by JAX's collectives and lax.ppermute only.
A program may use at most 192 MiB of HBM per device.

v0:
```python
import functools

import jax
import jax.numpy as jnp
from jax import lax
from jax.experimental import pallas as pl
from jax.experimental.pallas import tpu as pltpu
from jax.sharding import PartitionSpec as P

CLASSES = 128
SLOTS = 4
ROWS = 40
NEG = -1.0e30
BOTH = ("dp", "rep")

STRIDE = {"x": 1, "y": 32, "z": 8}
ORDERS = ("xyz", "yzx", "zxy")
BF, F32 = jnp.bfloat16, jnp.float32


def moves(axis, target):
    stride = STRIDE[axis]
    pairs = []
    for d in range(128):
        at = d // stride % 4
        pairs.append((d, d + (target(at) - at) * stride))
    return pairs


def shift(value, axis, step):
    return lax.ppermute(value, BOTH, moves(axis, lambda at: (at + step) % 4))


def swap(value, axis, mask):
    return lax.ppermute(value, BOTH, moves(axis, lambda at: at ^ mask))


def dot_t(a, b):
    return lax.dot_general(a, b, (((1,), (1,)), ((), ())), preferred_element_type=F32)


def near(value):
    return pltpu.with_memory_space_constraint(value, pltpu.VMEM)


def far_off(value):
    return pltpu.with_memory_space_constraint(value, pltpu.HBM)


def grant(mib):
    return pltpu.CompilerParams(vmem_limit_bytes=mib << 20)


VMEM = pl.BlockSpec(memory_space=pltpu.VMEM)
HBM = pl.BlockSpec(memory_space=pltpu.HBM)


def iota(shape, dim):
    return lax.broadcasted_iota(jnp.int32, shape, dim)


def route_kernel(q_ref, probes_ref, c0_ref, c1_ref, c2_ref, code_ref, probes, sems):
    fetch = pltpu.make_async_copy(probes_ref, probes, sems.at[3])
    fetch.start()
    loads = []
    for k, c_ref in enumerate((c0_ref, c1_ref, c2_ref)):
        columns = q_ref.at[:, 256 * k : 256 * k + 256]
        loads.append(pltpu.make_async_copy(columns, c_ref.at[0:64, :], sems.at[k]))
        loads[k].start()
    fetch.wait()
    named = probes[...].astype(F32)
    eye = (iota((64, 64), 0) == iota((64, 64), 1)).astype(BF)
    cols = dot_t(eye, named.astype(BF))
    earlier = iota((64, 64), 0) < iota((64, 64), 1)
    ranks = []
    for p in range(8):
        same = jnp.zeros((64, 64), F32)
        for o in range(8):
            same += (cols[:, o : o + 1] == named[p : p + 1, :]).astype(F32)
        ranks.append(jnp.sum(jnp.where(earlier, same, 0.0), axis=0, keepdims=True))
    rank = jnp.concatenate(ranks, axis=0)
    code_ref[...] = 4.0 * cols + dot_t(eye, rank.astype(BF))
    spread = (iota((64, 128), 0) == iota((64, 128), 1) % 64).astype(BF)
    c0_ref[64:72, 0:128] = jnp.dot(named.astype(BF), spread, preferred_element_type=F32).astype(BF)
    c0_ref[64:72, 128:256] = jnp.dot(rank.astype(BF), spread, preferred_element_type=F32).astype(BF)
    for load in loads:
        load.wait()


def route(queries, probes_t):
    return pl.pallas_call(
        route_kernel,
        out_shape=[pltpu.VMEM((72, 256), BF)]
        + [pltpu.VMEM((64, 256), BF)] * 2
        + [pltpu.VMEM((64, 8), F32)],
        in_specs=[HBM] * 2,
        out_specs=[VMEM] * 4,
        scratch_shapes=[pltpu.VMEM((8, 64), jnp.int32), pltpu.SemaphoreType.DMA((4,))],
        compiler_params=grant(4),
        name="route",
    )(far_off(queries), far_off(probes_t))


def join_kernel(a_ref, b_ref, out_ref):
    size = a_ref.shape[0]
    out_ref[0:size] = a_ref[...]
    out_ref[size : 2 * size] = b_ref[...]


def join(a, b):
    return pl.pallas_call(
        join_kernel,
        out_shape=pltpu.VMEM((2 * a.shape[0],) + a.shape[1:], a.dtype),
        in_specs=[VMEM] * 2,
        out_specs=VMEM,
        compiler_params=grant(4),
        name="join",
    )(near(a), near(b))


def half_kernel(at, a_ref, out_ref):
    out_ref[...] = a_ref[at : at + out_ref.shape[0]]


def half(a, at):
    return pl.pallas_call(
        functools.partial(half_kernel, at),
        out_shape=pltpu.VMEM((a.shape[0] // 2,) + a.shape[1:], a.dtype),
        in_specs=[VMEM],
        out_specs=VMEM,
        compiler_params=grant(4),
        name="half",
    )(near(a))


def gather(chunks):
    held = [c[None] for c in chunks]
    for stage in range(2):
        axes = [ORDERS[k][stage] for k in range(3)]
        for mask in (1, 3):
            other = [swap(held[k], axes[k], mask) for k in range(3)]
            for k in range(3):
                held[k] = join(held[k], other[k])
    axes = [ORDERS[k][2] for k in range(3)]
    up = [shift(held[k], axes[k], -1) for k in range(3)]
    down = [shift(held[k], axes[k], 1) for k in range(3)]
    half_a, half_b = [], []
    for k in range(3):
        half_a.append(half(up[k], 0))
        half_b.append(half(down[k], 8))
    far_a = [shift(half_a[k], axes[k], -1) for k in range(3)]
    far_b = [shift(half_b[k], axes[k], 1) for k in range(3)]
    return [(held[k], up[k], far_a[k], far_b[k], down[k]) for k in range(3)]


def position():
    dp, x = lax.axis_index("dp"), lax.axis_index("rep")
    return dp, (x, dp // 8, dp // 2 % 4), dp % 2


def pick_kernel(*refs):
    dp, here, _ = position()
    coords = [[(me + r) % 4 for r in range(4)] for me in here]
    apart = [[at ^ me for at in ats] for ats, me in zip(coords, here)]
    place = [[d ^ (d >> 1) for d in ds] for ds in apart]
    pieces = [refs[5 * k : 5 * k + 5] for k in range(3)]
    own_ref, other_ref, *far = refs[15:]
    for k in range(3):
        far[k][0:8] = pieces[k][2][...]
        far[k][8:16] = pieces[k][3][...]
    lane = iota((16, 256), 1) // 64
    row = iota((16, 256), 0)
    source = jnp.where(
        lane == 0,
        coords[0][0],
        jnp.where(lane == 1, coords[0][1], jnp.where(lane == 2, coords[0][2], coords[0][3])),
    )
    want = jnp.where(row // 4 == source, row % 4 + 1, -1).astype(F32)
    part = iota((8, 128), 1) // 64
    cluster = iota((8, 256), 0)
    bases = [(dp * 8 + cluster).astype(F32), ((dp ^ 1) * 8 + cluster).astype(F32)]

    def block(k, rx, ry, rz, aux):
        r = (rx, ry, rz)
        order = ["xyz".index(a) for a in ORDERS[k]]
        at = place[order[1]][r[order[1]]] * 4 + place[order[0]][r[order[0]]]
        last = r[order[2]]
        rows = slice(64, 72) if aux else slice(0, 64)
        if last == 2:
            return far[k][at, rows, :]
        return pieces[k][{0: 0, 1: 1, 3: 4}[last]][at, rows, :]

    def pair(a, b):
        return jnp.where(part < 1, a, b)

    def aux_of(blocks, columns):
        a = [b[:, columns] for b in blocks]
        return jnp.concatenate([pair(a[0], a[1]), pair(a[2], a[3])], axis=1)

    for ry in range(4):
        for rz in range(4):
            blocks = [block(0, rx, ry, rz, True).astype(F32) for rx in range(4)]
            probe = aux_of(blocks, slice(0, 128))
            rank = aux_of(blocks, slice(128, 256))
            picks = []
            for g in range(2):
                slot = jnp.zeros((8, 256), F32)
                for p in range(8):
                    slot += jnp.where(probe[p : p + 1, :] == bases[g], rank[p : p + 1, :] + 1.0, 0.0)
                for c in range(8):
                    picks.append(jnp.where(slot[c : c + 1, :] == want, 2.0, 0.0).astype(BF))
            pick = jnp.concatenate(picks, axis=0)
            base = pl.multiple_of((coords[1][ry] * 4 + coords[2][rz]) * 16, 16)
            for k in range(3):
                rows = jnp.concatenate([block(k, rx, ry, rz, False) for rx in range(4)], axis=0)
                found = jnp.dot(pick, rows, preferred_element_type=F32).astype(BF)
                for c in range(8):
                    own_ref[c, pl.ds(base, 16), 256 * k : 256 * k + 256] = found[16 * c : 16 * c + 16]
                    other_ref[c, pl.ds(base, 16), 256 * k : 256 * k + 256] = found[
                        128 + 16 * c : 144 + 16 * c
                    ]


def pick(pieces):
    flat = [near(a) for p in pieces for a in p]
    out = pltpu.VMEM((8, 256, 768), BF)
    return pl.pallas_call(
        pick_kernel,
        out_shape=(out, out),
        in_specs=[VMEM] * 15,
        out_specs=(VMEM, VMEM),
        scratch_shapes=[pltpu.VMEM((16,) + p[0].shape[1:], BF) for p in pieces],
        compiler_params=grant(12),
        name="pick",
    )(*flat)


def score_body(p_ref, bank_ref, labels_ref, acc, tal, wide, shifts, even, odd):
    clusters = p_ref.shape[0]
    lane = iota((64, 128), 1) - lax.axis_index("rep") * 32
    shifts[...] = jnp.zeros_like(shifts)

    def begin(c, held):
        tops = []
        for rows in (slice(r, r + 256) for r in range(0, 1024, 256)):
            s = dot_t(bank_ref[c, rows, :], p_ref[c])
            held[rows, :] = s
            tops.append(jnp.max(s, axis=0, keepdims=True))
        return jnp.maximum(jnp.maximum(tops[0], tops[1]), jnp.maximum(tops[2], tops[3]))

    def finish(c, held, top):
        high = top.astype(BF).astype(F32)
        m = high + (top - high).astype(BF).astype(F32)
        e = jnp.exp(held[...] - m).astype(BF)
        onehot = (labels_ref[pl.ds(c, 1), :] == iota((CLASSES, 1024), 0)).astype(F32).astype(BF)
        tal[...] = jnp.dot(onehot, e, preferred_element_type=F32).T
        wide[...] = jnp.broadcast_to(m, (128, 256)).T
        for j in range(SLOTS):
            acc[pl.ds(c * SLOTS + j, 64, stride=ROWS), :] = tal[pl.ds(j, 64, stride=SLOTS), :]
            shifts[...] = jnp.where(
                lane == c * SLOTS + j, wide[pl.ds(j, 64, stride=SLOTS), :], shifts[...]
            )

    def two(n, top):
        c = 2 * n
        other = begin(c + 1, odd)
        finish(c, even, top)
        top = begin(c + 2, even)
        finish(c + 1, odd, other)
        return top

    top = begin(0, even)
    for n in range(clusters // 2 - 1):
        top = two(n, top)
    other = begin(clusters - 1, odd)
    finish(clusters - 2, even, top)
    finish(clusters - 1, odd, other)
    full = shifts[...]
    first = full.astype(BF).astype(F32)
    acc[pl.ds(32, 64, stride=ROWS), :] = first
    acc[pl.ds(33, 64, stride=ROWS), :] = full - first
    for j in range(34, ROWS):
        acc[pl.ds(j, 64, stride=ROWS), :] = jnp.zeros((64, 128), F32)


def score_own_kernel(p_ref, bank_ref, labels_ref, out_ref, *scratch):
    score_body(p_ref, bank_ref, labels_ref, *scratch)
    out_ref[...] = scratch[0][...].astype(BF)


def score_other_kernel(p_ref, bank_ref, labels_ref, own_ref, out_ref, *scratch):
    score_body(p_ref, bank_ref, labels_ref, *scratch)
    acc, core = scratch[0], position()[2]
    size = 4 * ROWS
    for yz in range(16):
        mine = pl.multiple_of((yz * 2 + core) * size, 16)
        theirs = pl.multiple_of((yz * 2 + 1 - core) * size, 16)
        out_ref[pl.ds(mine, size), :] = own_ref[yz * size : yz * size + size, :]
        out_ref[pl.ds(theirs, size), :] = acc[yz * size : yz * size + size, :].astype(BF)


def score(picked, bank, labels, own=None):
    clusters, rows, width = bank.shape
    count = picked.shape[1]
    args = [near(picked), near(bank), near(labels)]
    out_rows = 64 * ROWS
    if own is not None:
        args.append(near(own))
        out_rows = 128 * ROWS
    return pl.pallas_call(
        score_own_kernel if own is None else score_other_kernel,
        out_shape=pltpu.VMEM((out_rows, 128), BF),
        in_specs=[VMEM] * len(args),
        out_specs=VMEM,
        scratch_shapes=[
            pltpu.VMEM((64 * ROWS, 128), F32),
            pltpu.VMEM((256, 128), F32),
            pltpu.VMEM((256, 128), F32),
            pltpu.VMEM((64, 128), F32),
            pltpu.VMEM((1024, 256), F32),
            pltpu.VMEM((1024, 256), F32),
        ],
        compiler_params=grant(12),
        cost_estimate=pl.CostEstimate(
            flops=2 * clusters * count * rows * (width + 128),
            transcendentals=clusters * count * rows,
            bytes_accessed=bank.size * 2,
        ),
        name="score_own" if own is None else "score_other",
    )(*args)


def marks_kernel(code_ref, marks_ref):
    slot = (iota((64, 128), 1) % 32).astype(F32)
    codes = [jnp.broadcast_to(code_ref[:, p : p + 1], (64, 128)) for p in range(8)]
    for g in range(32):
        here = slot + 32.0 * g
        hit = codes[0] == here
        for p in range(1, 8):
            hit = jnp.logical_or(hit, codes[p] == here)
        marks_ref[g] = jnp.where(hit, 0.0, NEG)


def marks_of(codes):
    return pl.pallas_call(
        marks_kernel,
        out_shape=pltpu.VMEM((32, 64, 128), F32),
        in_specs=[VMEM],
        out_specs=VMEM,
        compiler_params=grant(4),
        name="marks",
    )(near(codes))


def fold_kernel(marks_ref, parts_ref, out_ref, marked):
    best = jnp.full((64, 128), NEG, F32)
    for g in range(32):
        rows = parts_ref[4 * g, 32:40, :].astype(F32)
        for r in range(1, 4):
            rows += parts_ref[4 * g + r, 32:40, :].astype(F32)
        m = rows[0:1, :] + rows[1:2, :]
        value = marks_ref[g] + m
        marked[g] = value
        best = jnp.maximum(best, value)
    top = jnp.max(best, axis=1, keepdims=True)
    total = jnp.zeros((128, 128), F32)
    for g in range(0, 32, 2):
        pair = []
        for h in range(2):
            w = jnp.exp(marked[g + h] - top)
            first = w.astype(BF)
            pair.append(jnp.concatenate([first, (w - first.astype(F32)).astype(BF)], axis=0))
        weights = jnp.concatenate(pair, axis=1)
        tallies = jnp.concatenate([parts_ref[4 * g + r, 0:32, :] for r in range(8)], axis=0)
        total += jnp.dot(weights, tallies, preferred_element_type=F32)
    votes = total[0:64] + total[64:128]
    out_ref[...] = CLASSES * votes / jnp.sum(votes, axis=1, keepdims=True)


def fold(marks, parts):
    return pl.pallas_call(
        fold_kernel,
        out_shape=jax.ShapeDtypeStruct((64, CLASSES), F32),
        in_specs=[VMEM] * 2,
        out_specs=VMEM,
        scratch_shapes=[pltpu.VMEM((32, 64, 128), F32)],
        compiler_params=grant(8),
        name="fold",
    )(near(marks), near(parts))


def local(queries, bank, labels, probes):
    *chunks, codes = route(queries, probes.T)
    pieces = gather(chunks)
    marks = marks_of(codes)
    own, other = pick(pieces)
    arrived = lax.ppermute(other, BOTH, [(d, d ^ 4) for d in range(128)])
    mine = score(own, bank, labels)
    blocks = score(arrived, bank, labels, mine)
    parts = lax.all_to_all(
        blocks.reshape(128, ROWS, 128), BOTH, split_axis=0, concat_axis=0, tiled=True
    )
    return fold(marks, parts)


def solution(mesh):
    return jax.shard_map(
        local,
        mesh=mesh,
        in_specs=(
            P(BOTH, None),
            P("dp", "rep", None),
            P("dp", "rep"),
            P(BOTH, None),
        ),
        out_specs=P(BOTH, None),
        check_vma=False,
    )
```

profile of v0, /device:TPU:1, one launch (start us, length us, event | category | flops | bytes accessed | tf_op | source)
XLA Modules:
  0.0 123.7 jit_solution(4231479288473636376)
XLA Ops:
  0.0 1.3 %route.1 = (bf16[72,256]{1,0:T(8,128)(2,1)S(1)}, bf16[64,256]{1,0:T(8,128)(2,1)S(1)}, bf16[64,256]{1,0:T(8,128)(2,1)S(1)}, f32[64,8]{1,0:T(8,128)S(1)}) custom-call(bf16[64,768]{1,0:T(8,128)(2,1)} %q_ref.1, s32[8,64]{1,0:T(8,128)} %bitcast.11), custom_call_target="tpu_custom_call" | custom-call | tf_op jit(solution)/shard_map/route/pallas_call | solution.py:91
  1.3 2.2 %collective-permute-start.8 = (bf16[1,64,256]{2,1,0:T(8,128)(2,1)S(1)}, bf16[1,64,256]{2,1,0:T(8,128)(2,1)S(1)}, u32[]{:S(2)}, u32[]{:S(2)}) collective-permute-start(bf16[1,64,256]{2,1,0:T(8,128)(2,1)S(1)} %bitcast.9), channel_id=1, source_target_pairs={{0,32},{1,33},{2,34},{3,35},{4,36},{5,37},{6,38},{7,39},{8,40},{9,... | collective-permute-start | bytes 98312 | tf_op jit(solution)/shard_map/ppermute | solution.py:35
  3.5 1.3 %collective-permute-done.8.b_ref = bf16[1,64,256]{2,1,0:T(8,128)(2,1)S(1)} collective-permute-done((bf16[1,64,256]{2,1,0:T(8,128)(2,1)S(1)}, bf16[1,64,256]{2,1,0:T(8,128)(2,1)S(1)}, u32[]{:S(2)}, u32[]{:S(2)}) %collective-permute-start.8) | collective-permute-done | bytes 32800 | tf_op jit(solution)/shard_map/ppermute | solution.py:35
  4.8 2.9 %collective-permute-start.9 = (bf16[2,64,256]{2,1,0:T(8,128)(2,1)S(1)}, bf16[2,64,256]{2,1,0:T(8,128)(2,1)S(1)}, u32[]{:S(2)}, u32[]{:S(2)}) collective-permute-start(bf16[2,64,256]{2,1,0:T(8,128)(2,1)S(1)} %join.16.a_ref), channel_id=1, source_target_pairs={{0,96},{1,97},{2,98},{3,99},{4,100},{5,101},{6,102},{7,103},{8,104... | collective-permute-start | bytes 196616 | tf_op jit(solution)/shard_map/ppermute | solution.py:35
  7.7 1.7 %collective-permute-done.9.b_ref = bf16[2,64,256]{2,1,0:T(8,128)(2,1)S(1)} collective-permute-done((bf16[2,64,256]{2,1,0:T(8,128)(2,1)S(1)}, bf16[2,64,256]{2,1,0:T(8,128)(2,1)S(1)}, u32[]{:S(2)}, u32[]{:S(2)}) %collective-permute-start.9) | collective-permute-done | bytes 65568 | tf_op jit(solution)/shard_map/ppermute | solution.py:35
  9.4 1.7 %collective-permute-start.10 = (bf16[4,64,256]{2,1,0:T(8,128)(2,1)S(1)}, bf16[4,64,256]{2,1,0:T(8,128)(2,1)S(1)}, u32[]{:S(2)}, u32[]{:S(2)}) collective-permute-start(bf16[4,64,256]{2,1,0:T(8,128)(2,1)S(1)} %join.17.a_ref), channel_id=1, source_target_pairs={{0,8},{1,9},{2,10},{3,11},{4,12},{5,13},{6,14},{7,15},{8,0},{9,1},... | collective-permute-start | bytes 393224 | tf_op jit(solution)/shard_map/ppermute | solution.py:35
  11.1 1.2 collective-permute-start
  12.3 1.6 %collective-permute-done.b_ref = bf16[1,72,256]{2,1,0:T(8,128)(2,1)S(1)} collective-permute-done((bf16[1,72,256]{2,1,0:T(8,128)(2,1)S(1)}, bf16[1,72,256]{2,1,0:T(8,128)(2,1)S(1)}, u32[]{:S(2)}, u32[]{:S(2)}) %collective-permute-start) | collective-permute-done | bytes 36896 | tf_op jit(solution)/shard_map/ppermute | solution.py:35
  13.9 2.5 %collective-permute-start.1 = (bf16[2,72,256]{2,1,0:T(8,128)(2,1)S(1)}, bf16[2,72,256]{2,1,0:T(8,128)(2,1)S(1)}, u32[]{:S(2)}, u32[]{:S(2)}) collective-permute-start(bf16[2,72,256]{2,1,0:T(8,128)(2,1)S(1)} %join.12.a_ref), channel_id=1, source_target_pairs={{0,3},{1,2},{2,1},{3,0},{4,7},{5,6},{6,5},{7,4},{8,11},{9,10},{10,... | collective-permute-start | bytes 221192 | tf_op jit(solution)/shard_map/ppermute | solution.py:35
  16.4 0.0 collective-permute-done.10.b_ref
  16.4 2.3 %collective-permute-start.11 = (bf16[8,64,256]{2,1,0:T(8,128)(2,1)S(1)}, bf16[8,64,256]{2,1,0:T(8,128)(2,1)S(1)}, u32[]{:S(2)}, u32[]{:S(2)}) collective-permute-start(bf16[8,64,256]{2,1,0:T(8,128)(2,1)S(1)} %join.18.a_ref), channel_id=1, source_target_pairs={{0,24},{1,25},{2,26},{3,27},{4,28},{5,29},{6,30},{7,31},{8,16},{9,... | collective-permute-start | bytes 786440 | tf_op jit(solution)/shard_map/ppermute | solution.py:35
  18.7 0.0 collective-permute-done.1.b_ref
  18.7 0.1 collective-permute-start.2
  18.8 4.3 %collective-permute-done.2.b_ref = bf16[4,72,256]{2,1,0:T(8,128)(2,1)S(1)} collective-permute-done((bf16[4,72,256]{2,1,0:T(8,128)(2,1)S(1)}, bf16[4,72,256]{2,1,0:T(8,128)(2,1)S(1)}, u32[]{:S(2)}, u32[]{:S(2)}) %collective-permute-start.2) | collective-permute-done | bytes 147488 | tf_op jit(solution)/shard_map/ppermute | solution.py:35
  23.1 2.8 %collective-permute-start.3 = (bf16[8,72,256]{2,1,0:T(8,128)(2,1)S(1)}, bf16[8,72,256]{2,1,0:T(8,128)(2,1)S(1)}, u32[]{:S(2)}, u32[]{:S(2)}) collective-permute-start(bf16[8,72,256]{2,1,0:T(8,128)(2,1)S(1)} %join.14.a_ref), channel_id=1, source_target_pairs={{0,96},{1,97},{2,98},{3,99},{4,100},{5,101},{6,102},{7,103},{8,104... | collective-permute-start | bytes 884744 | tf_op jit(solution)/shard_map/ppermute | solution.py:35
  25.9 0.0 collective-permute-done.11.b_ref
  25.9 0.1 collective-permute-start.14
  26.0 0.5 collective-permute-start.16
  26.5 2.3 %collective-permute-done.16.b_ref = bf16[1,64,256]{2,1,0:T(8,128)(2,1)S(1)} collective-permute-done((bf16[1,64,256]{2,1,0:T(8,128)(2,1)S(1)}, bf16[1,64,256]{2,1,0:T(8,128)(2,1)S(1)}, u32[]{:S(2)}, u32[]{:S(2)}) %collective-permute-start.16) | collective-permute-done | bytes 32800 | tf_op jit(solution)/shard_map/ppermute | solution.py:35
  28.9 2.0 %collective-permute-start.17 = (bf16[2,64,256]{2,1,0:T(8,128)(2,1)S(1)}, bf16[2,64,256]{2,1,0:T(8,128)(2,1)S(1)}, u32[]{:S(2)}, u32[]{:S(2)}) collective-permute-start(bf16[2,64,256]{2,1,0:T(8,128)(2,1)S(1)} %join.20.a_ref), channel_id=1, source_target_pairs={{0,24},{1,25},{2,26},{3,27},{4,28},{5,29},{6,30},{7,31},{8,16},{9,... | collective-permute-start | bytes 196616 | tf_op jit(solution)/shard_map/ppermute | solution.py:35
  30.9 2.3 %collective-permute-done.17.b_ref = bf16[2,64,256]{2,1,0:T(8,128)(2,1)S(1)} collective-permute-done((bf16[2,64,256]{2,1,0:T(8,128)(2,1)S(1)}, bf16[2,64,256]{2,1,0:T(8,128)(2,1)S(1)}, u32[]{:S(2)}, u32[]{:S(2)}) %collective-permute-start.17) | collective-permute-done | bytes 65568 | tf_op jit(solution)/shard_map/ppermute | solution.py:35
  33.2 1.1 collective-permute-start.18
  34.3 0.0 collective-permute-done.3.b_ref
  34.3 0.5 collective-permute-start.6
  34.9 2.7 %collective-permute-done.18.b_ref = bf16[4,64,256]{2,1,0:T(8,128)(2,1)S(1)} collective-permute-done((bf16[4,64,256]{2,1,0:T(8,128)(2,1)S(1)}, bf16[4,64,256]{2,1,0:T(8,128)(2,1)S(1)}, u32[]{:S(2)}, u32[]{:S(2)}) %collective-permute-start.18) | collective-permute-done | bytes 131104 | tf_op jit(solution)/shard_map/ppermute | solution.py:35
  37.6 0.0 copy-start
  37.6 4.1 %collective-permute-start.19 = (bf16[8,64,256]{2,1,0:T(8,128)(2,1)S(1)}, bf16[8,64,256]{2,1,0:T(8,128)(2,1)S(1)}, u32[]{:S(2)}, u32[]{:S(2)}) collective-permute-start(bf16[8,64,256]{2,1,0:T(8,128)(2,1)S(1)} %join.22.a_ref), channel_id=1, source_target_pairs={{0,3},{1,2},{2,1},{3,0},{4,7},{5,6},{6,5},{7,4},{8,11},{9,10},{10,... | collective-permute-start | bytes 786440 | tf_op jit(solution)/shard_map/ppermute | solution.py:35
  41.8 1.6 %collective-permute-start.4 = (bf16[16,72,256]{2,1,0:T(8,128)(2,1)S(1)}, bf16[16,72,256]{2,1,0:T(8,128)(2,1)S(1)}, u32[]{:S(2)}, u32[]{:S(2)}) collective-permute-start(bf16[16,72,256]{2,1,0:T(8,128)(2,1)S(1)} %join.15.refs_0_), channel_id=1, source_target_pairs={{0,24},{1,25},{2,26},{3,27},{4,28},{5,29},{6,30},{7,31},{8,0},{9,1... | collective-permute-start | bytes 1769480 | tf_op jit(solution)/shard_map/ppermute | solution.py:31
  43.4 0.1 collective-permute-start.12
  43.5 2.0 %collective-permute-done.19.b_ref = bf16[8,64,256]{2,1,0:T(8,128)(2,1)S(1)} collective-permute-done((bf16[8,64,256]{2,1,0:T(8,128)(2,1)S(1)}, bf16[8,64,256]{2,1,0:T(8,128)(2,1)S(1)}, u32[]{:S(2)}, u32[]{:S(2)}) %collective-permute-start.19) | collective-permute-done | bytes 262176 | tf_op jit(solution)/shard_map/ppermute | solution.py:35
  45.6 0.1 collective-permute-start.22
  45.7 0.0 collective-permute-done.14.a_ref.refs_9_
  45.7 2.7 %collective-permute-start.20 = (bf16[16,64,256]{2,1,0:T(8,128)(2,1)S(1)}, bf16[16,64,256]{2,1,0:T(8,128)(2,1)S(1)}, u32[]{:S(2)}, u32[]{:S(2)}) collective-permute-start(bf16[16,64,256]{2,1,0:T(8,128)(2,1)S(1)} %join.23.refs_10_), channel_id=1, source_target_pairs={{0,96},{1,97},{2,98},{3,99},{4,100},{5,101},{6,102},{7,103},{8,104... | collective-permute-start | bytes 1572872 | tf_op jit(solution)/shard_map/ppermute | solution.py:31
  48.3 0.0 collective-permute-done.6.a_ref.refs_4_
  48.4 0.1 collective-permute-start.15
  48.5 2.3 %collective-permute-done.4.a_ref.refs_1_ = bf16[16,72,256]{2,1,0:T(8,128)(2,1)S(1)} collective-permute-done((bf16[16,72,256]{2,1,0:T(8,128)(2,1)S(1)}, bf16[16,72,256]{2,1,0:T(8,128)(2,1)S(1)}, u32[]{:S(2)}, u32[]{:S(2)}) %collective-permute-start.4) | collective-permute-done | bytes 589856 | tf_op jit(solution)/shard_map/ppermute | solution.py:31
  50.8 0.0 collective-permute-start.7
  50.8 2.1 %collective-permute-done.12.a_ref.refs_6_ = bf16[16,64,256]{2,1,0:T(8,128)(2,1)S(1)} collective-permute-done((bf16[16,64,256]{2,1,0:T(8,128)(2,1)S(1)}, bf16[16,64,256]{2,1,0:T(8,128)(2,1)S(1)}, u32[]{:S(2)}, u32[]{:S(2)}) %collective-permute-start.12) | collective-permute-done | bytes 524320 | tf_op jit(solution)/shard_map/ppermute | solution.py:31
  52.9 0.7 collective-permute-start.5
  53.6 1.6 %collective-permute-done.22.a_ref.refs_14_ = bf16[16,64,256]{2,1,0:T(8,128)(2,1)S(1)} collective-permute-done((bf16[16,64,256]{2,1,0:T(8,128)(2,1)S(1)}, bf16[16,64,256]{2,1,0:T(8,128)(2,1)S(1)}, u32[]{:S(2)}, u32[]{:S(2)}) %collective-permute-start.22) | collective-permute-done | bytes 524320 | tf_op jit(solution)/shard_map/ppermute | solution.py:31
  55.2 2.7 %collective-permute-start.13 = (bf16[8,64,256]{2,1,0:T(8,128)(2,1)S(1)}, bf16[8,64,256]{2,1,0:T(8,128)(2,1)S(1)}, u32[]{:S(2)}, u32[]{:S(2)}) collective-permute-start(bf16[8,64,256]{2,1,0:T(8,128)(2,1)S(1)} %half.8), channel_id=1, source_target_pairs={{0,3},{1,0},{2,1},{3,2},{4,7},{5,4},{6,5},{7,6},{8,11},{9,8},{10,9... | collective-permute-start | bytes 786440 | tf_op jit(solution)/shard_map/ppermute | solution.py:31
  57.9 0.0 collective-permute-done.20.a_ref.refs_11_
  57.9 0.1 collective-permute-start.23
  58.0 0.0 copy-start.1
  58.0 0.0 collective-permute-done.15.refs_8_
  58.0 2.7 %collective-permute-start.21 = (bf16[8,64,256]{2,1,0:T(8,128)(2,1)S(1)}, bf16[8,64,256]{2,1,0:T(8,128)(2,1)S(1)}, u32[]{:S(2)}, u32[]{:S(2)}) collective-permute-start(bf16[8,64,256]{2,1,0:T(8,128)(2,1)S(1)} %half.10), channel_id=1, source_target_pairs={{0,96},{1,97},{2,98},{3,99},{4,100},{5,101},{6,102},{7,103},{8,104... | collective-permute-start | bytes 786440 | tf_op jit(solution)/shard_map/ppermute | solution.py:31
  60.7 2.8 %collective-permute-done.13.refs_7_ = bf16[8,64,256]{2,1,0:T(8,128)(2,1)S(1)} collective-permute-done((bf16[8,64,256]{2,1,0:T(8,128)(2,1)S(1)}, bf16[8,64,256]{2,1,0:T(8,128)(2,1)S(1)}, u32[]{:S(2)}, u32[]{:S(2)}) %collective-permute-start.13) | collective-permute-done | bytes 262176 | tf_op jit(solution)/shard_map/ppermute | solution.py:31
  63.5 3.0 %collective-permute-done.23.refs_13_ = bf16[8,64,256]{2,1,0:T(8,128)(2,1)S(1)} collective-permute-done((bf16[8,64,256]{2,1,0:T(8,128)(2,1)S(1)}, bf16[8,64,256]{2,1,0:T(8,128)(2,1)S(1)}, u32[]{:S(2)}, u32[]{:S(2)}) %collective-permute-start.23) | collective-permute-done | bytes 262176 | tf_op jit(solution)/shard_map/ppermute | solution.py:31
  66.5 0.0 collective-permute-done.21.refs_12_
  66.5 0.0 collective-permute-done.7.refs_3_
  66.5 0.0 collective-permute-done.5.refs_2_
  66.5 1.9 %pick.1 = (bf16[8,256,768]{2,1,0:T(8,128)(2,1)S(1)}, bf16[8,256,768]{2,1,0:T(8,128)(2,1)S(1)}) custom-call(bf16[16,72,256]{2,1,0:T(8,128)(2,1)S(1)} %join.15.refs_0_, bf16[16,72,256]{2,1,0:T(8,128)(2,1)S(1)} %collective-permute-done.4.a_ref.refs_1_, bf16[8,72,256]{2,1,0:T(8,128)(2,1)S(1)} %collective-permute-done.5.refs_2_, ...), custom_call_target="tpu_custom_call" | custom-call | tf_op jit(solution)/shard_map/pick/pallas_call | solution.py:227
  68.5 12.4 %collective-permute-start.24 = (bf16[8,256,768]{2,1,0:T(8,128)(2,1)S(1)}, bf16[8,256,768]{2,1,0:T(8,128)(2,1)S(1)}, u32[]{:S(2)}, u32[]{:S(2)}) collective-permute-start(bf16[8,256,768]{2,1,0:T(8,128)(2,1)S(1)} %get-tuple-element.15), channel_id=1, source_target_pairs={{0,4},{1,5},{2,6},{3,7},{4,0},{5,1},{6,2},{7,3},{8,12},{9,13},{10,... | collective-permute-start | bytes 9437192 | tf_op jit(solution)/shard_map/ppermute | solution.py:397
  80.9 0.0 copy-done
  80.9 0.0 copy-done.1
  80.9 5.4 %score_own.1.own_ref = bf16[2560,128]{1,0:T(8,128)(2,1)S(1)} custom-call(bf16[8,256,768]{2,1,0:T(8,128)(2,1)S(1)} %get-tuple-element.16.p_ref, bf16[8,1024,768]{2,1,0:T(8,128)(2,1)S(1)} %copy-done, s32[8,1024]{1,0:T(8,128)S(1)} %copy-done.1), custom_call_target="tpu_custom_call" | custom-call | flops 3758096384 | bytes 12582912 | tf_op jit(solution)/shard_map/score_own/pallas_call | solution.py:310
  86.3 0.0 collective-permute-done.24.p_ref
  86.3 6.5 %score_other.1 = bf16[5120,128]{1,0:T(8,128)(2,1)} custom-call(bf16[8,256,768]{2,1,0:T(8,128)(2,1)S(1)} %collective-permute-done.24.p_ref, bf16[8,1024,768]{2,1,0:T(8,128)(2,1)S(1)} %copy-done, s32[8,1024]{1,0:T(8,128)S(1)} %copy-done.1, bf16[2560,128]{1,0:T(8,128)(2,1)S(1)} %score_own.1.own_ref), custom_call_target="tpu_custom_call" | custom-call | flops 3758096384 | bytes 12582912 | tf_op jit(solution)/shard_map/score_other/pallas_call | solution.py:310
  92.8 7.0 %all-to-all-start = ((bf16[128,40,128]{2,1,0:T(8,128)(2,1)}), bf16[128,40,128]{2,1,0:T(8,128)(2,1)S(1)}, u32[]{:S(2)}, u32[]{:S(2)}) async-start(bf16[128,40,128]{2,1,0:T(8,128)(2,1)} %bitcast.4), calls=%async_computation | async-start | bytes 2621440 | tf_op jit(solution)/shard_map/all_to_all | solution.py:400
  99.8 1.4 %marks.1.marks_ref = f32[32,64,128]{2,1,0:T(8,128)S(1)} custom-call(f32[64,8]{1,0:T(8,128)S(1)} %get-tuple-element.11.code_ref), custom_call_target="tpu_custom_call" | custom-call | tf_op jit(solution)/shard_map/marks/pallas_call | solution.py:345
  101.2 21.1 %all-to-all-done.parts_ref = bf16[128,40,128]{2,1,0:T(8,128)(2,1)S(1)} async-done(((bf16[128,40,128]{2,1,0:T(8,128)(2,1)}), bf16[128,40,128]{2,1,0:T(8,128)(2,1)S(1)}, u32[]{:S(2)}, u32[]{:S(2)}) %all-to-all-start) | async-done | bytes 1310752 | tf_op jit(solution)/shard_map/all_to_all | solution.py:400
  122.3 1.3 %fold.1 = f32[64,128]{1,0:T(8,128)} custom-call(f32[32,64,128]{2,1,0:T(8,128)S(1)} %marks.1.marks_ref, bf16[128,40,128]{2,1,0:T(8,128)(2,1)S(1)} %all-to-all-done.parts_ref), custom_call_target="tpu_custom_call" | custom-call | tf_op jit(solution)/shard_map/fold/pallas_call | solution.py:381
  (18 shorter events, 0.3 us)
Async XLA Ops:
  1.3 3.5 %collective-permute-start.8 = (bf16[1,64,256]{2,1,0:T(8,128)(2,1)S(1)}, bf16[1,64,256]{2,1,0:T(8,128)(2,1)S(1)}, u32[]{:S(2)}, u32[]{:S(2)}) collective-permute-start(bf16[1,64,256]{2,1,0:T(8,128)(2,1)S(1)} %bitcast.9), channel_id=1, source_target_pairs={{0,32},{1,33},{2,34},{3,35},{4,36},{5,37},{6,38},{7,39},{8,40},{9,... | collective-permute-start | bytes 98312 | tf_op jit(solution)/shard_map/ppermute | solution.py:35
  4.8 4.6 %collective-permute-start.9 = (bf16[2,64,256]{2,1,0:T(8,128)(2,1)S(1)}, bf16[2,64,256]{2,1,0:T(8,128)(2,1)S(1)}, u32[]{:S(2)}, u32[]{:S(2)}) collective-permute-start(bf16[2,64,256]{2,1,0:T(8,128)(2,1)S(1)} %join.16.a_ref), channel_id=1, source_target_pairs={{0,96},{1,97},{2,98},{3,99},{4,100},{5,101},{6,102},{7,103},{8,104... | collective-permute-start | bytes 196616 | tf_op jit(solution)/shard_map/ppermute | solution.py:35
  9.4 7.0 %collective-permute-start.10 = (bf16[4,64,256]{2,1,0:T(8,128)(2,1)S(1)}, bf16[4,64,256]{2,1,0:T(8,128)(2,1)S(1)}, u32[]{:S(2)}, u32[]{:S(2)}) collective-permute-start(bf16[4,64,256]{2,1,0:T(8,128)(2,1)S(1)} %join.17.a_ref), channel_id=1, source_target_pairs={{0,8},{1,9},{2,10},{3,11},{4,12},{5,13},{6,14},{7,15},{8,0},{9,1},... | collective-permute-start | bytes 393224 | tf_op jit(solution)/shard_map/ppermute | solution.py:35
  11.1 2.8 %collective-permute-start = (bf16[1,72,256]{2,1,0:T(8,128)(2,1)S(1)}, bf16[1,72,256]{2,1,0:T(8,128)(2,1)S(1)}, u32[]{:S(2)}, u32[]{:S(2)}) collective-permute-start(bf16[1,72,256]{2,1,0:T(8,128)(2,1)S(1)} %bitcast.5), channel_id=1, source_target_pairs={{0,1},{1,0},{2,3},{3,2},{4,5},{5,4},{6,7},{7,6},{8,9},{9,8},{10,11... | collective-permute-start | bytes 110600 | tf_op jit(solution)/shard_map/ppermute | solution.py:35
  13.9 4.8 %collective-permute-start.1 = (bf16[2,72,256]{2,1,0:T(8,128)(2,1)S(1)}, bf16[2,72,256]{2,1,0:T(8,128)(2,1)S(1)}, u32[]{:S(2)}, u32[]{:S(2)}) collective-permute-start(bf16[2,72,256]{2,1,0:T(8,128)(2,1)S(1)} %join.12.a_ref), channel_id=1, source_target_pairs={{0,3},{1,2},{2,1},{3,0},{4,7},{5,6},{6,5},{7,4},{8,11},{9,10},{10,... | collective-permute-start | bytes 221192 | tf_op jit(solution)/shard_map/ppermute | solution.py:35
  16.4 9.5 %collective-permute-start.11 = (bf16[8,64,256]{2,1,0:T(8,128)(2,1)S(1)}, bf16[8,64,256]{2,1,0:T(8,128)(2,1)S(1)}, u32[]{:S(2)}, u32[]{:S(2)}) collective-permute-start(bf16[8,64,256]{2,1,0:T(8,128)(2,1)S(1)} %join.18.a_ref), channel_id=1, source_target_pairs={{0,24},{1,25},{2,26},{3,27},{4,28},{5,29},{6,30},{7,31},{8,16},{9,... | collective-permute-start | bytes 786440 | tf_op jit(solution)/shard_map/ppermute | solution.py:35
  18.7 4.4 %collective-permute-start.2 = (bf16[4,72,256]{2,1,0:T(8,128)(2,1)S(1)}, bf16[4,72,256]{2,1,0:T(8,128)(2,1)S(1)}, u32[]{:S(2)}, u32[]{:S(2)}) collective-permute-start(bf16[4,72,256]{2,1,0:T(8,128)(2,1)S(1)} %join.13.a_ref), channel_id=1, source_target_pairs={{0,32},{1,33},{2,34},{3,35},{4,36},{5,37},{6,38},{7,39},{8,40},{9,... | collective-permute-start | bytes 442376 | tf_op jit(solution)/shard_map/ppermute | solution.py:35
  23.1 11.2 %collective-permute-start.3 = (bf16[8,72,256]{2,1,0:T(8,128)(2,1)S(1)}, bf16[8,72,256]{2,1,0:T(8,128)(2,1)S(1)}, u32[]{:S(2)}, u32[]{:S(2)}) collective-permute-start(bf16[8,72,256]{2,1,0:T(8,128)(2,1)S(1)} %join.14.a_ref), channel_id=1, source_target_pairs={{0,96},{1,97},{2,98},{3,99},{4,100},{5,101},{6,102},{7,103},{8,104... | collective-permute-start | bytes 884744 | tf_op jit(solution)/shard_map/ppermute | solution.py:35
  25.9 19.7 %collective-permute-start.14 = (bf16[16,64,256]{2,1,0:T(8,128)(2,1)S(1)}, bf16[16,64,256]{2,1,0:T(8,128)(2,1)S(1)}, u32[]{:S(2)}, u32[]{:S(2)}) collective-permute-start(bf16[16,64,256]{2,1,0:T(8,128)(2,1)S(1)} %join.19.refs_5_), channel_id=1, source_target_pairs={{0,1},{1,2},{2,3},{3,0},{4,5},{5,6},{6,7},{7,4},{8,9},{9,10},{10,1... | collective-permute-start | bytes 1572872 | tf_op jit(solution)/shard_map/ppermute | solution.py:31
  26.0 2.8 %collective-permute-start.16 = (bf16[1,64,256]{2,1,0:T(8,128)(2,1)S(1)}, bf16[1,64,256]{2,1,0:T(8,128)(2,1)S(1)}, u32[]{:S(2)}, u32[]{:S(2)}) collective-permute-start(bf16[1,64,256]{2,1,0:T(8,128)(2,1)S(1)} %bitcast.7), channel_id=1, source_target_pairs={{0,8},{1,9},{2,10},{3,11},{4,12},{5,13},{6,14},{7,15},{8,0},{9,1},... | collective-permute-start | bytes 98312 | tf_op jit(solution)/shard_map/ppermute | solution.py:35
  28.9 4.3 %collective-permute-start.17 = (bf16[2,64,256]{2,1,0:T(8,128)(2,1)S(1)}, bf16[2,64,256]{2,1,0:T(8,128)(2,1)S(1)}, u32[]{:S(2)}, u32[]{:S(2)}) collective-permute-start(bf16[2,64,256]{2,1,0:T(8,128)(2,1)S(1)} %join.20.a_ref), channel_id=1, source_target_pairs={{0,24},{1,25},{2,26},{3,27},{4,28},{5,29},{6,30},{7,31},{8,16},{9,... | collective-permute-start | bytes 196616 | tf_op jit(solution)/shard_map/ppermute | solution.py:35
  33.2 4.4 %collective-permute-start.18 = (bf16[4,64,256]{2,1,0:T(8,128)(2,1)S(1)}, bf16[4,64,256]{2,1,0:T(8,128)(2,1)S(1)}, u32[]{:S(2)}, u32[]{:S(2)}) collective-permute-start(bf16[4,64,256]{2,1,0:T(8,128)(2,1)S(1)} %join.21.a_ref), channel_id=1, source_target_pairs={{0,1},{1,0},{2,3},{3,2},{4,5},{5,4},{6,7},{7,6},{8,9},{9,8},{10,11... | collective-permute-start | bytes 393224 | tf_op jit(solution)/shard_map/ppermute | solution.py:35
  34.3 14.0 %collective-permute-start.6 = (bf16[16,72,256]{2,1,0:T(8,128)(2,1)S(1)}, bf16[16,72,256]{2,1,0:T(8,128)(2,1)S(1)}, u32[]{:S(2)}, u32[]{:S(2)}) collective-permute-start(bf16[16,72,256]{2,1,0:T(8,128)(2,1)S(1)} %join.15.refs_0_), channel_id=1, source_target_pairs={{0,8},{1,9},{2,10},{3,11},{4,12},{5,13},{6,14},{7,15},{8,16},{9,17... | collective-permute-start | bytes 1769480 | tf_op jit(solution)/shard_map/ppermute | solution.py:31
  37.6 43.3 %copy-start = (bf16[8,1024,768]{2,1,0:T(8,128)(2,1)S(1)}, bf16[8,1024,768]{2,1,0:T(8,128)(2,1)}, u32[]{:S(2)}) copy-start(bf16[8,1024,768]{2,1,0:T(8,128)(2,1)} %bank_ref.3) | copy-start | bytes 37748740
  37.6 7.9 %collective-permute-start.19 = (bf16[8,64,256]{2,1,0:T(8,128)(2,1)S(1)}, bf16[8,64,256]{2,1,0:T(8,128)(2,1)S(1)}, u32[]{:S(2)}, u32[]{:S(2)}) collective-permute-start(bf16[8,64,256]{2,1,0:T(8,128)(2,1)S(1)} %join.22.a_ref), channel_id=1, source_target_pairs={{0,3},{1,2},{2,1},{3,0},{4,7},{5,6},{6,5},{7,4},{8,11},{9,10},{10,... | collective-permute-start | bytes 786440 | tf_op jit(solution)/shard_map/ppermute | solution.py:35
  41.8 9.0 %collective-permute-start.4 = (bf16[16,72,256]{2,1,0:T(8,128)(2,1)S(1)}, bf16[16,72,256]{2,1,0:T(8,128)(2,1)S(1)}, u32[]{:S(2)}, u32[]{:S(2)}) collective-permute-start(bf16[16,72,256]{2,1,0:T(8,128)(2,1)S(1)} %join.15.refs_0_), channel_id=1, source_target_pairs={{0,24},{1,25},{2,26},{3,27},{4,28},{5,29},{6,30},{7,31},{8,0},{9,1... | collective-permute-start | bytes 1769480 | tf_op jit(solution)/shard_map/ppermute | solution.py:31
  43.4 9.5 %collective-permute-start.12 = (bf16[16,64,256]{2,1,0:T(8,128)(2,1)S(1)}, bf16[16,64,256]{2,1,0:T(8,128)(2,1)S(1)}, u32[]{:S(2)}, u32[]{:S(2)}) collective-permute-start(bf16[16,64,256]{2,1,0:T(8,128)(2,1)S(1)} %join.19.refs_5_), channel_id=1, source_target_pairs={{0,3},{1,0},{2,1},{3,2},{4,7},{5,4},{6,5},{7,6},{8,11},{9,8},{10,9... | collective-permute-start | bytes 1572872 | tf_op jit(solution)/shard_map/ppermute | solution.py:31
  45.6 9.6 %collective-permute-start.22 = (bf16[16,64,256]{2,1,0:T(8,128)(2,1)S(1)}, bf16[16,64,256]{2,1,0:T(8,128)(2,1)S(1)}, u32[]{:S(2)}, u32[]{:S(2)}) collective-permute-start(bf16[16,64,256]{2,1,0:T(8,128)(2,1)S(1)} %join.23.refs_10_), channel_id=1, source_target_pairs={{0,32},{1,33},{2,34},{3,35},{4,36},{5,37},{6,38},{7,39},{8,40},{9,... | collective-permute-start | bytes 1572872 | tf_op jit(solution)/shard_map/ppermute | solution.py:31
  45.7 12.2 %collective-permute-start.20 = (bf16[16,64,256]{2,1,0:T(8,128)(2,1)S(1)}, bf16[16,64,256]{2,1,0:T(8,128)(2,1)S(1)}, u32[]{:S(2)}, u32[]{:S(2)}) collective-permute-start(bf16[16,64,256]{2,1,0:T(8,128)(2,1)S(1)} %join.23.refs_10_), channel_id=1, source_target_pairs={{0,96},{1,97},{2,98},{3,99},{4,100},{5,101},{6,102},{7,103},{8,104... | collective-permute-start | bytes 1572872 | tf_op jit(solution)/shard_map/ppermute | solution.py:31
  48.4 9.7 %collective-permute-start.15 = (bf16[8,64,256]{2,1,0:T(8,128)(2,1)S(1)}, bf16[8,64,256]{2,1,0:T(8,128)(2,1)S(1)}, u32[]{:S(2)}, u32[]{:S(2)}) collective-permute-start(bf16[8,64,256]{2,1,0:T(8,128)(2,1)S(1)} %half.9), channel_id=1, source_target_pairs={{0,1},{1,2},{2,3},{3,0},{4,5},{5,6},{6,7},{7,4},{8,9},{9,10},{10,1... | collective-permute-start | bytes 786440 | tf_op jit(solution)/shard_map/ppermute | solution.py:31
  50.8 15.7 %collective-permute-start.7 = (bf16[8,72,256]{2,1,0:T(8,128)(2,1)S(1)}, bf16[8,72,256]{2,1,0:T(8,128)(2,1)S(1)}, u32[]{:S(2)}, u32[]{:S(2)}) collective-permute-start(bf16[8,72,256]{2,1,0:T(8,128)(2,1)S(1)} %half.7), channel_id=1, source_target_pairs={{0,8},{1,9},{2,10},{3,11},{4,12},{5,13},{6,14},{7,15},{8,16},{9,17... | collective-permute-start | bytes 884744 | tf_op jit(solution)/shard_map/ppermute | solution.py:31
  52.9 13.6 %collective-permute-start.5 = (bf16[8,72,256]{2,1,0:T(8,128)(2,1)S(1)}, bf16[8,72,256]{2,1,0:T(8,128)(2,1)S(1)}, u32[]{:S(2)}, u32[]{:S(2)}) collective-permute-start(bf16[8,72,256]{2,1,0:T(8,128)(2,1)S(1)} %half.6), channel_id=1, source_target_pairs={{0,24},{1,25},{2,26},{3,27},{4,28},{5,29},{6,30},{7,31},{8,0},{9,1... | collective-permute-start | bytes 884744 | tf_op jit(solution)/shard_map/ppermute | solution.py:31
  55.2 8.3 %collective-permute-start.13 = (bf16[8,64,256]{2,1,0:T(8,128)(2,1)S(1)}, bf16[8,64,256]{2,1,0:T(8,128)(2,1)S(1)}, u32[]{:S(2)}, u32[]{:S(2)}) collective-permute-start(bf16[8,64,256]{2,1,0:T(8,128)(2,1)S(1)} %half.8), channel_id=1, source_target_pairs={{0,3},{1,0},{2,1},{3,2},{4,7},{5,4},{6,5},{7,6},{8,11},{9,8},{10,9... | collective-permute-start | bytes 786440 | tf_op jit(solution)/shard_map/ppermute | solution.py:31
  57.9 8.6 %collective-permute-start.23 = (bf16[8,64,256]{2,1,0:T(8,128)(2,1)S(1)}, bf16[8,64,256]{2,1,0:T(8,128)(2,1)S(1)}, u32[]{:S(2)}, u32[]{:S(2)}) collective-permute-start(bf16[8,64,256]{2,1,0:T(8,128)(2,1)S(1)} %half.11), channel_id=1, source_target_pairs={{0,32},{1,33},{2,34},{3,35},{4,36},{5,37},{6,38},{7,39},{8,40},{9,... | collective-permute-start | bytes 786440 | tf_op jit(solution)/shard_map/ppermute | solution.py:31
  58.0 22.9 %copy-start.1 = (s32[8,1024]{1,0:T(8,128)S(1)}, s32[8,1024]{1,0:T(8,128)}, u32[]{:S(2)}) copy-start(s32[8,1024]{1,0:T(8,128)} %labels_ref.3) | copy-start | bytes 98308
  58.0 8.5 %collective-permute-start.21 = (bf16[8,64,256]{2,1,0:T(8,128)(2,1)S(1)}, bf16[8,64,256]{2,1,0:T(8,128)(2,1)S(1)}, u32[]{:S(2)}, u32[]{:S(2)}) collective-permute-start(bf16[8,64,256]{2,1,0:T(8,128)(2,1)S(1)} %half.10), channel_id=1, source_target_pairs={{0,96},{1,97},{2,98},{3,99},{4,100},{5,101},{6,102},{7,103},{8,104... | collective-permute-start | bytes 786440 | tf_op jit(solution)/shard_map/ppermute | solution.py:31
  68.5 17.8 %collective-permute-start.24 = (bf16[8,256,768]{2,1,0:T(8,128)(2,1)S(1)}, bf16[8,256,768]{2,1,0:T(8,128)(2,1)S(1)}, u32[]{:S(2)}, u32[]{:S(2)}) collective-permute-start(bf16[8,256,768]{2,1,0:T(8,128)(2,1)S(1)} %get-tuple-element.15), channel_id=1, source_target_pairs={{0,4},{1,5},{2,6},{3,7},{4,0},{5,1},{6,2},{7,3},{8,12},{9,13},{10,... | collective-permute-start | bytes 9437192 | tf_op jit(solution)/shard_map/ppermute | solution.py:397
  92.8 29.5 %all-to-all-start = ((bf16[128,40,128]{2,1,0:T(8,128)(2,1)}), bf16[128,40,128]{2,1,0:T(8,128)(2,1)S(1)}, u32[]{:S(2)}, u32[]{:S(2)}) async-start(bf16[128,40,128]{2,1,0:T(8,128)(2,1)} %bitcast.4), calls=%async_computation | async-start | bytes 2621440 | tf_op jit(solution)/shard_map/all_to_all | solution.py:400
where the time goes:
time: 124 us
  starting transfers between devices  54.1 us (44%)
  waiting for transfers between devices  51.1 us (41%)
  Pallas kernels  18.2 us (15%)
    ppermute x12, starting transfers between devices, swap(): return lax.ppermute(value, BOTH, moves(axis, lambda at: at ^ mask))  23.5 us
    all_to_all x1, waiting for transfers between devices, local(): lax.all_to_all(blocks.reshape(128, ROWS, 128), BOTH, split_axis=0, concat...  21.1 us
    ppermute x12, waiting for transfers between devices, swap(): return lax.ppermute(value, BOTH, moves(axis, lambda at: at ^ mask))  18.2 us
    ppermute x1, starting transfers between devices, local(): arrived = lax.ppermute(other, BOTH, [(d, d ^ 4) for d in range(128)])  12.4 us
    pallas_call x2, Pallas kernels, score(): pl.pallas_call(score_own_kernel if own is None else score_other_kernel, o...  11.9 us
    ppermute x12, waiting for transfers between devices, shift(): return lax.ppermute(value, BOTH, moves(axis, lambda at: (at + step) % 4))  11.8 us
    ppermute x12, starting transfers between devices, shift(): return lax.ppermute(value, BOTH, moves(axis, lambda at: (at + step) % 4))  11.3 us
    all_to_all x1, starting transfers between devices, local(): lax.all_to_all(blocks.reshape(128, ROWS, 128), BOTH, split_axis=0, concat...  6.99 us
  transfers between devices with their start and end apart: 26, of which 14 were waited for; matrix products, arithmetic and copies ran while one was open for 0% of the time, Pallas kernels for 6%

commit v1 on v0

--- a/solution.py
+++ b/solution.py
@@ -79,7 +79,8 @@
             same += (cols[:, o : o + 1] == named[p : p + 1, :]).astype(F32)
         ranks.append(jnp.sum(jnp.where(earlier, same, 0.0), axis=0, keepdims=True))
     rank = jnp.concatenate(ranks, axis=0)
-    code_ref[...] = 4.0 * cols + dot_t(eye, rank.astype(BF))
+    code_ref[0:8, :] = named
+    code_ref[8:16, :] = rank
     spread = (iota((64, 128), 0) == iota((64, 128), 1) % 64).astype(BF)
     c0_ref[64:72, 0:128] = jnp.dot(named.astype(BF), spread, preferred_element_type=F32).astype(BF)
     c0_ref[64:72, 128:256] = jnp.dot(rank.astype(BF), spread, preferred_element_type=F32).astype(BF)
@@ -92,7 +93,7 @@
         route_kernel,
         out_shape=[pltpu.VMEM((72, 256), BF)]
         + [pltpu.VMEM((64, 256), BF)] * 2
-        + [pltpu.VMEM((64, 8), F32)],
+        + [pltpu.VMEM((16, 64), F32)],
         in_specs=[HBM] * 2,
         out_specs=[VMEM] * 4,
         scratch_shapes=[pltpu.VMEM((8, 64), jnp.int32), pltpu.SemaphoreType.DMA((4,))],
@@ -332,7 +333,10 @@
 
 def marks_kernel(code_ref, marks_ref):
     slot = (iota((64, 128), 1) % 32).astype(F32)
-    codes = [jnp.broadcast_to(code_ref[:, p : p + 1], (64, 128)) for p in range(8)]
+    eye = (iota((64, 64), 0) == iota((64, 64), 1)).astype(BF)
+    both = dot_t(eye, code_ref[...].astype(BF))
+    code = 4.0 * both[:, 0:8] + both[:, 8:16]
+    codes = [jnp.broadcast_to(code[:, p : p + 1], (64, 128)) for p in range(8)]
     for g in range(32):
         here = slot + 32.0 * g
         hit = codes[0] == here

time: 124 us -> 124 us (level)
  no operation moved by 1% of the time
where the time goes in v1:
time: 124 us
  starting transfers between devices  54.1 us (44%)
  waiting for transfers between devices  51.1 us (41%)
  Pallas kernels  18.2 us (15%)
    ppermute x12, starting transfers between devices, swap(): return lax.ppermute(value, BOTH, moves(axis, lambda at: at ^ mask))  23.5 us
    all_to_all x1, waiting for transfers between devices, local(): lax.all_to_all(blocks.reshape(128, ROWS, 128), BOTH, split_axis=0, concat...  21.1 us
    ppermute x12, waiting for transfers between devices, swap(): return lax.ppermute(value, BOTH, moves(axis, lambda at: at ^ mask))  18.2 us
    ppermute x1, starting transfers between devices, local(): arrived = lax.ppermute(other, BOTH, [(d, d ^ 4) for d in range(128)])  12.4 us
    pallas_call x2, Pallas kernels, score(): pl.pallas_call(score_own_kernel if own is None else score_other_kernel, o...  11.9 us
    ppermute x12, waiting for transfers between devices, shift(): return lax.ppermute(value, BOTH, moves(axis, lambda at: (at + step) % 4))  11.8 us
    ppermute x12, starting transfers between devices, shift(): return lax.ppermute(value, BOTH, moves(axis, lambda at: (at + step) % 4))  11.3 us
    all_to_all x1, starting transfers between devices, local(): lax.all_to_all(blocks.reshape(128, ROWS, 128), BOTH, split_axis=0, concat...  7.01 us
  transfers between devices with their start and end apart: 26, of which 14 were waited for; matrix products, arithmetic and copies ran while one was open for 0% of the time, Pallas kernels for 6%

profile of v1, /device:TPU:1, one launch (start us, length us, event | category | flops | bytes accessed | tf_op | source)
XLA Modules:
  0.0 123.7 jit_solution(9707661029603533421)
XLA Ops:
  0.0 1.3 %route.1 = (bf16[72,256]{1,0:T(8,128)(2,1)S(1)}, bf16[64,256]{1,0:T(8,128)(2,1)S(1)}, bf16[64,256]{1,0:T(8,128)(2,1)S(1)}, f32[16,64]{1,0:T(8,128)S(1)}) custom-call(bf16[64,768]{1,0:T(8,128)(2,1)} %q_ref.1, s32[8,64]{1,0:T(8,128)} %bitcast.11), custom_call_target="tpu_custom_call" | custom-call | tf_op jit(solution)/shard_map/route/pallas_call | solution.py:92
  1.3 2.2 %collective-permute-start.8 = (bf16[1,64,256]{2,1,0:T(8,128)(2,1)S(1)}, bf16[1,64,256]{2,1,0:T(8,128)(2,1)S(1)}, u32[]{:S(2)}, u32[]{:S(2)}) collective-permute-start(bf16[1,64,256]{2,1,0:T(8,128)(2,1)S(1)} %bitcast.9), channel_id=1, source_target_pairs={{0,32},{1,33},{2,34},{3,35},{4,36},{5,37},{6,38},{7,39},{8,40},{9,... | collective-permute-start | bytes 98312 | tf_op jit(solution)/shard_map/ppermute | solution.py:35
  3.5 1.3 %collective-permute-done.8.b_ref = bf16[1,64,256]{2,1,0:T(8,128)(2,1)S(1)} collective-permute-done((bf16[1,64,256]{2,1,0:T(8,128)(2,1)S(1)}, bf16[1,64,256]{2,1,0:T(8,128)(2,1)S(1)}, u32[]{:S(2)}, u32[]{:S(2)}) %collective-permute-start.8) | collective-permute-done | bytes 32800 | tf_op jit(solution)/shard_map/ppermute | solution.py:35
  4.8 2.9 %collective-permute-start.9 = (bf16[2,64,256]{2,1,0:T(8,128)(2,1)S(1)}, bf16[2,64,256]{2,1,0:T(8,128)(2,1)S(1)}, u32[]{:S(2)}, u32[]{:S(2)}) collective-permute-start(bf16[2,64,256]{2,1,0:T(8,128)(2,1)S(1)} %join.16.a_ref), channel_id=1, source_target_pairs={{0,96},{1,97},{2,98},{3,99},{4,100},{5,101},{6,102},{7,103},{8,104... | collective-permute-start | bytes 196616 | tf_op jit(solution)/shard_map/ppermute | solution.py:35
  7.7 1.7 %collective-permute-done.9.b_ref = bf16[2,64,256]{2,1,0:T(8,128)(2,1)S(1)} collective-permute-done((bf16[2,64,256]{2,1,0:T(8,128)(2,1)S(1)}, bf16[2,64,256]{2,1,0:T(8,128)(2,1)S(1)}, u32[]{:S(2)}, u32[]{:S(2)}) %collective-permute-start.9) | collective-permute-done | bytes 65568 | tf_op jit(solution)/shard_map/ppermute | solution.py:35
  9.3 1.7 %collective-permute-start.10 = (bf16[4,64,256]{2,1,0:T(8,128)(2,1)S(1)}, bf16[4,64,256]{2,1,0:T(8,128)(2,1)S(1)}, u32[]{:S(2)}, u32[]{:S(2)}) collective-permute-start(bf16[4,64,256]{2,1,0:T(8,128)(2,1)S(1)} %join.17.a_ref), channel_id=1, source_target_pairs={{0,8},{1,9},{2,10},{3,11},{4,12},{5,13},{6,14},{7,15},{8,0},{9,1},... | collective-permute-start | bytes 393224 | tf_op jit(solution)/shard_map/ppermute | solution.py:35
  11.1 1.2 collective-permute-start
  12.3 1.6 %collective-permute-done.b_ref = bf16[1,72,256]{2,1,0:T(8,128)(2,1)S(1)} collective-permute-done((bf16[1,72,256]{2,1,0:T(8,128)(2,1)S(1)}, bf16[1,72,256]{2,1,0:T(8,128)(2,1)S(1)}, u32[]{:S(2)}, u32[]{:S(2)}) %collective-permute-start) | collective-permute-done | bytes 36896 | tf_op jit(solution)/shard_map/ppermute | solution.py:35
  13.9 2.5 %collective-permute-start.1 = (bf16[2,72,256]{2,1,0:T(8,128)(2,1)S(1)}, bf16[2,72,256]{2,1,0:T(8,128)(2,1)S(1)}, u32[]{:S(2)}, u32[]{:S(2)}) collective-permute-start(bf16[2,72,256]{2,1,0:T(8,128)(2,1)S(1)} %join.12.a_ref), channel_id=1, source_target_pairs={{0,3},{1,2},{2,1},{3,0},{4,7},{5,6},{6,5},{7,4},{8,11},{9,10},{10,... | collective-permute-start | bytes 221192 | tf_op jit(solution)/shard_map/ppermute | solution.py:35
  16.4 0.0 collective-permute-done.10.b_ref
  16.4 2.3 %collective-permute-start.11 = (bf16[8,64,256]{2,1,0:T(8,128)(2,1)S(1)}, bf16[8,64,256]{2,1,0:T(8,128)(2,1)S(1)}, u32[]{:S(2)}, u32[]{:S(2)}) collective-permute-start(bf16[8,64,256]{2,1,0:T(8,128)(2,1)S(1)} %join.18.a_ref), channel_id=1, source_target_pairs={{0,24},{1,25},{2,26},{3,27},{4,28},{5,29},{6,30},{7,31},{8,16},{9,... | collective-permute-start | bytes 786440 | tf_op jit(solution)/shard_map/ppermute | solution.py:35
  18.7 0.0 collective-permute-done.1.b_ref
  18.7 0.1 collective-permute-start.2
  18.8 4.3 %collective-permute-done.2.b_ref = bf16[4,72,256]{2,1,0:T(8,128)(2,1)S(1)} collective-permute-done((bf16[4,72,256]{2,1,0:T(8,128)(2,1)S(1)}, bf16[4,72,256]{2,1,0:T(8,128)(2,1)S(1)}, u32[]{:S(2)}, u32[]{:S(2)}) %collective-permute-start.2) | collective-permute-done | bytes 147488 | tf_op jit(solution)/shard_map/ppermute | solution.py:35
  23.1 2.8 %collective-permute-start.3 = (bf16[8,72,256]{2,1,0:T(8,128)(2,1)S(1)}, bf16[8,72,256]{2,1,0:T(8,128)(2,1)S(1)}, u32[]{:S(2)}, u32[]{:S(2)}) collective-permute-start(bf16[8,72,256]{2,1,0:T(8,128)(2,1)S(1)} %join.14.a_ref), channel_id=1, source_target_pairs={{0,96},{1,97},{2,98},{3,99},{4,100},{5,101},{6,102},{7,103},{8,104... | collective-permute-start | bytes 884744 | tf_op jit(solution)/shard_map/ppermute | solution.py:35
  25.9 0.0 collective-permute-done.11.b_ref
  25.9 0.1 collective-permute-start.14
  26.0 0.5 collective-permute-start.16
  26.5 2.3 %collective-permute-done.16.b_ref = bf16[1,64,256]{2,1,0:T(8,128)(2,1)S(1)} collective-permute-done((bf16[1,64,256]{2,1,0:T(8,128)(2,1)S(1)}, bf16[1,64,256]{2,1,0:T(8,128)(2,1)S(1)}, u32[]{:S(2)}, u32[]{:S(2)}) %collective-permute-start.16) | collective-permute-done | bytes 32800 | tf_op jit(solution)/shard_map/ppermute | solution.py:35
  28.8 2.0 %collective-permute-start.17 = (bf16[2,64,256]{2,1,0:T(8,128)(2,1)S(1)}, bf16[2,64,256]{2,1,0:T(8,128)(2,1)S(1)}, u32[]{:S(2)}, u32[]{:S(2)}) collective-permute-start(bf16[2,64,256]{2,1,0:T(8,128)(2,1)S(1)} %join.20.a_ref), channel_id=1, source_target_pairs={{0,24},{1,25},{2,26},{3,27},{4,28},{5,29},{6,30},{7,31},{8,16},{9,... | collective-permute-start | bytes 196616 | tf_op jit(solution)/shard_map/ppermute | solution.py:35
  30.9 2.3 %collective-permute-done.17.b_ref = bf16[2,64,256]{2,1,0:T(8,128)(2,1)S(1)} collective-permute-done((bf16[2,64,256]{2,1,0:T(8,128)(2,1)S(1)}, bf16[2,64,256]{2,1,0:T(8,128)(2,1)S(1)}, u32[]{:S(2)}, u32[]{:S(2)}) %collective-permute-start.17) | collective-permute-done | bytes 65568 | tf_op jit(solution)/shard_map/ppermute | solution.py:35
  33.2 1.1 collective-permute-start.18
  34.3 0.0 collective-permute-done.3.b_ref
  34.3 0.5 collective-permute-start.6
  34.9 2.7 %collective-permute-done.18.b_ref = bf16[4,64,256]{2,1,0:T(8,128)(2,1)S(1)} collective-permute-done((bf16[4,64,256]{2,1,0:T(8,128)(2,1)S(1)}, bf16[4,64,256]{2,1,0:T(8,128)(2,1)S(1)}, u32[]{:S(2)}, u32[]{:S(2)}) %collective-permute-start.18) | collective-permute-done | bytes 131104 | tf_op jit(solution)/shard_map/ppermute | solution.py:35
  37.6 0.0 copy-start
  37.6 4.1 %collective-permute-start.19 = (bf16[8,64,256]{2,1,0:T(8,128)(2,1)S(1)}, bf16[8,64,256]{2,1,0:T(8,128)(2,1)S(1)}, u32[]{:S(2)}, u32[]{:S(2)}) collective-permute-start(bf16[8,64,256]{2,1,0:T(8,128)(2,1)S(1)} %join.22.a_ref), channel_id=1, source_target_pairs={{0,3},{1,2},{2,1},{3,0},{4,7},{5,6},{6,5},{7,4},{8,11},{9,10},{10,... | collective-permute-start | bytes 786440 | tf_op jit(solution)/shard_map/ppermute | solution.py:35
  41.8 1.6 %collective-permute-start.4 = (bf16[16,72,256]{2,1,0:T(8,128)(2,1)S(1)}, bf16[16,72,256]{2,1,0:T(8,128)(2,1)S(1)}, u32[]{:S(2)}, u32[]{:S(2)}) collective-permute-start(bf16[16,72,256]{2,1,0:T(8,128)(2,1)S(1)} %join.15.refs_0_), channel_id=1, source_target_pairs={{0,24},{1,25},{2,26},{3,27},{4,28},{5,29},{6,30},{7,31},{8,0},{9,1... | collective-permute-start | bytes 1769480 | tf_op jit(solution)/shard_map/ppermute | solution.py:31
  43.4 0.1 collective-permute-start.12
  43.5 2.0 %collective-permute-done.19.b_ref = bf16[8,64,256]{2,1,0:T(8,128)(2,1)S(1)} collective-permute-done((bf16[8,64,256]{2,1,0:T(8,128)(2,1)S(1)}, bf16[8,64,256]{2,1,0:T(8,128)(2,1)S(1)}, u32[]{:S(2)}, u32[]{:S(2)}) %collective-permute-start.19) | collective-permute-done | bytes 262176 | tf_op jit(solution)/shard_map/ppermute | solution.py:35
  45.6 0.1 collective-permute-start.22
  45.6 0.0 collective-permute-done.14.a_ref.refs_9_
  45.7 2.7 %collective-permute-start.20 = (bf16[16,64,256]{2,1,0:T(8,128)(2,1)S(1)}, bf16[16,64,256]{2,1,0:T(8,128)(2,1)S(1)}, u32[]{:S(2)}, u32[]{:S(2)}) collective-permute-start(bf16[16,64,256]{2,1,0:T(8,128)(2,1)S(1)} %join.23.refs_10_), channel_id=1, source_target_pairs={{0,96},{1,97},{2,98},{3,99},{4,100},{5,101},{6,102},{7,103},{8,104... | collective-permute-start | bytes 1572872 | tf_op jit(solution)/shard_map/ppermute | solution.py:31
  48.3 0.0 collective-permute-done.6.a_ref.refs_4_
  48.3 0.1 collective-permute-start.15
  48.5 2.3 %collective-permute-done.4.a_ref.refs_1_ = bf16[16,72,256]{2,1,0:T(8,128)(2,1)S(1)} collective-permute-done((bf16[16,72,256]{2,1,0:T(8,128)(2,1)S(1)}, bf16[16,72,256]{2,1,0:T(8,128)(2,1)S(1)}, u32[]{:S(2)}, u32[]{:S(2)}) %collective-permute-start.4) | collective-permute-done | bytes 589856 | tf_op jit(solution)/shard_map/ppermute | solution.py:31
  50.8 0.0 collective-permute-start.7
  50.8 2.1 %collective-permute-done.12.a_ref.refs_6_ = bf16[16,64,256]{2,1,0:T(8,128)(2,1)S(1)} collective-permute-done((bf16[16,64,256]{2,1,0:T(8,128)(2,1)S(1)}, bf16[16,64,256]{2,1,0:T(8,128)(2,1)S(1)}, u32[]{:S(2)}, u32[]{:S(2)}) %collective-permute-start.12) | collective-permute-done | bytes 524320 | tf_op jit(solution)/shard_map/ppermute | solution.py:31
  52.9 0.7 collective-permute-start.5
  53.6 1.6 %collective-permute-done.22.a_ref.refs_14_ = bf16[16,64,256]{2,1,0:T(8,128)(2,1)S(1)} collective-permute-done((bf16[16,64,256]{2,1,0:T(8,128)(2,1)S(1)}, bf16[16,64,256]{2,1,0:T(8,128)(2,1)S(1)}, u32[]{:S(2)}, u32[]{:S(2)}) %collective-permute-start.22) | collective-permute-done | bytes 524320 | tf_op jit(solution)/shard_map/ppermute | solution.py:31
  55.2 2.7 %collective-permute-start.13 = (bf16[8,64,256]{2,1,0:T(8,128)(2,1)S(1)}, bf16[8,64,256]{2,1,0:T(8,128)(2,1)S(1)}, u32[]{:S(2)}, u32[]{:S(2)}) collective-permute-start(bf16[8,64,256]{2,1,0:T(8,128)(2,1)S(1)} %half.8), channel_id=1, source_target_pairs={{0,3},{1,0},{2,1},{3,2},{4,7},{5,4},{6,5},{7,6},{8,11},{9,8},{10,9... | collective-permute-start | bytes 786440 | tf_op jit(solution)/shard_map/ppermute | solution.py:31
  57.9 0.0 collective-permute-done.20.a_ref.refs_11_
  57.9 0.1 collective-permute-start.23
  58.0 0.0 copy-start.1
  58.0 0.0 collective-permute-done.15.refs_8_
  58.0 2.7 %collective-permute-start.21 = (bf16[8,64,256]{2,1,0:T(8,128)(2,1)S(1)}, bf16[8,64,256]{2,1,0:T(8,128)(2,1)S(1)}, u32[]{:S(2)}, u32[]{:S(2)}) collective-permute-start(bf16[8,64,256]{2,1,0:T(8,128)(2,1)S(1)} %half.10), channel_id=1, source_target_pairs={{0,96},{1,97},{2,98},{3,99},{4,100},{5,101},{6,102},{7,103},{8,104... | collective-permute-start | bytes 786440 | tf_op jit(solution)/shard_map/ppermute | solution.py:31
  60.7 2.8 %collective-permute-done.13.refs_7_ = bf16[8,64,256]{2,1,0:T(8,128)(2,1)S(1)} collective-permute-done((bf16[8,64,256]{2,1,0:T(8,128)(2,1)S(1)}, bf16[8,64,256]{2,1,0:T(8,128)(2,1)S(1)}, u32[]{:S(2)}, u32[]{:S(2)}) %collective-permute-start.13) | collective-permute-done | bytes 262176 | tf_op jit(solution)/shard_map/ppermute | solution.py:31
  63.5 3.0 %collective-permute-done.23.refs_13_ = bf16[8,64,256]{2,1,0:T(8,128)(2,1)S(1)} collective-permute-done((bf16[8,64,256]{2,1,0:T(8,128)(2,1)S(1)}, bf16[8,64,256]{2,1,0:T(8,128)(2,1)S(1)}, u32[]{:S(2)}, u32[]{:S(2)}) %collective-permute-start.23) | collective-permute-done | bytes 262176 | tf_op jit(solution)/shard_map/ppermute | solution.py:31
  66.5 0.0 collective-permute-done.21.refs_12_
  66.5 0.0 collective-permute-done.7.refs_3_
  66.5 0.0 collective-permute-done.5.refs_2_
  66.5 1.9 %pick.1 = (bf16[8,256,768]{2,1,0:T(8,128)(2,1)S(1)}, bf16[8,256,768]{2,1,0:T(8,128)(2,1)S(1)}) custom-call(bf16[16,72,256]{2,1,0:T(8,128)(2,1)S(1)} %join.15.refs_0_, bf16[16,72,256]{2,1,0:T(8,128)(2,1)S(1)} %collective-permute-done.4.a_ref.refs_1_, bf16[8,72,256]{2,1,0:T(8,128)(2,1)S(1)} %collective-permute-done.5.refs_2_, ...), custom_call_target="tpu_custom_call" | custom-call | tf_op jit(solution)/shard_map/pick/pallas_call | solution.py:228
  68.5 12.4 %collective-permute-start.24 = (bf16[8,256,768]{2,1,0:T(8,128)(2,1)S(1)}, bf16[8,256,768]{2,1,0:T(8,128)(2,1)S(1)}, u32[]{:S(2)}, u32[]{:S(2)}) collective-permute-start(bf16[8,256,768]{2,1,0:T(8,128)(2,1)S(1)} %get-tuple-element.15), channel_id=1, source_target_pairs={{0,4},{1,5},{2,6},{3,7},{4,0},{5,1},{6,2},{7,3},{8,12},{9,13},{10,... | collective-permute-start | bytes 9437192 | tf_op jit(solution)/shard_map/ppermute | solution.py:401
  80.9 0.0 copy-done
  80.9 0.0 copy-done.1
  80.9 5.4 %score_own.1.own_ref = bf16[2560,128]{1,0:T(8,128)(2,1)S(1)} custom-call(bf16[8,256,768]{2,1,0:T(8,128)(2,1)S(1)} %get-tuple-element.16.p_ref, bf16[8,1024,768]{2,1,0:T(8,128)(2,1)S(1)} %copy-done, s32[8,1024]{1,0:T(8,128)S(1)} %copy-done.1), custom_call_target="tpu_custom_call" | custom-call | flops 3758096384 | bytes 12582912 | tf_op jit(solution)/shard_map/score_own/pallas_call | solution.py:311
  86.3 0.0 collective-permute-done.24.p_ref
  86.3 6.5 %score_other.1 = bf16[5120,128]{1,0:T(8,128)(2,1)} custom-call(bf16[8,256,768]{2,1,0:T(8,128)(2,1)S(1)} %collective-permute-done.24.p_ref, bf16[8,1024,768]{2,1,0:T(8,128)(2,1)S(1)} %copy-done, s32[8,1024]{1,0:T(8,128)S(1)} %copy-done.1, bf16[2560,128]{1,0:T(8,128)(2,1)S(1)} %score_own.1.own_ref), custom_call_target="tpu_custom_call" | custom-call | flops 3758096384 | bytes 12582912 | tf_op jit(solution)/shard_map/score_other/pallas_call | solution.py:311
  92.8 7.0 %all-to-all-start = ((bf16[128,40,128]{2,1,0:T(8,128)(2,1)}), bf16[128,40,128]{2,1,0:T(8,128)(2,1)S(1)}, u32[]{:S(2)}, u32[]{:S(2)}) async-start(bf16[128,40,128]{2,1,0:T(8,128)(2,1)} %bitcast.4), calls=%async_computation | async-start | bytes 2621440 | tf_op jit(solution)/shard_map/all_to_all | solution.py:404
  99.8 1.5 %marks.1.marks_ref = f32[32,64,128]{2,1,0:T(8,128)S(1)} custom-call(f32[16,64]{1,0:T(8,128)S(1)} %get-tuple-element.11.code_ref), custom_call_target="tpu_custom_call" | custom-call | tf_op jit(solution)/shard_map/marks/pallas_call | solution.py:349
  101.3 21.1 %all-to-all-done.parts_ref = bf16[128,40,128]{2,1,0:T(8,128)(2,1)S(1)} async-done(((bf16[128,40,128]{2,1,0:T(8,128)(2,1)}), bf16[128,40,128]{2,1,0:T(8,128)(2,1)S(1)}, u32[]{:S(2)}, u32[]{:S(2)}) %all-to-all-start) | async-done | bytes 1310752 | tf_op jit(solution)/shard_map/all_to_all | solution.py:404
  122.3 1.3 %fold.1 = f32[64,128]{1,0:T(8,128)} custom-call(f32[32,64,128]{2,1,0:T(8,128)S(1)} %marks.1.marks_ref, bf16[128,40,128]{2,1,0:T(8,128)(2,1)S(1)} %all-to-all-done.parts_ref), custom_call_target="tpu_custom_call" | custom-call | tf_op jit(solution)/shard_map/fold/pallas_call | solution.py:385
  (18 shorter events, 0.3 us)
Async XLA Ops:
  1.3 3.5 %collective-permute-start.8 = (bf16[1,64,256]{2,1,0:T(8,128)(2,1)S(1)}, bf16[1,64,256]{2,1,0:T(8,128)(2,1)S(1)}, u32[]{:S(2)}, u32[]{:S(2)}) collective-permute-start(bf16[1,64,256]{2,1,0:T(8,128)(2,1)S(1)} %bitcast.9), channel_id=1, source_target_pairs={{0,32},{1,33},{2,34},{3,35},{4,36},{5,37},{6,38},{7,39},{8,40},{9,... | collective-permute-start | bytes 98312 | tf_op jit(solution)/shard_map/ppermute | solution.py:35
  4.8 4.6 %collective-permute-start.9 = (bf16[2,64,256]{2,1,0:T(8,128)(2,1)S(1)}, bf16[2,64,256]{2,1,0:T(8,128)(2,1)S(1)}, u32[]{:S(2)}, u32[]{:S(2)}) collective-permute-start(bf16[2,64,256]{2,1,0:T(8,128)(2,1)S(1)} %join.16.a_ref), channel_id=1, source_target_pairs={{0,96},{1,97},{2,98},{3,99},{4,100},{5,101},{6,102},{7,103},{8,104... | collective-permute-start | bytes 196616 | tf_op jit(solution)/shard_map/ppermute | solution.py:35
  9.3 7.0 %collective-permute-start.10 = (bf16[4,64,256]{2,1,0:T(8,128)(2,1)S(1)}, bf16[4,64,256]{2,1,0:T(8,128)(2,1)S(1)}, u32[]{:S(2)}, u32[]{:S(2)}) collective-permute-start(bf16[4,64,256]{2,1,0:T(8,128)(2,1)S(1)} %join.17.a_ref), channel_id=1, source_target_pairs={{0,8},{1,9},{2,10},{3,11},{4,12},{5,13},{6,14},{7,15},{8,0},{9,1},... | collective-permute-start | bytes 393224 | tf_op jit(solution)/shard_map/ppermute | solution.py:35
  11.1 2.8 %collective-permute-start = (bf16[1,72,256]{2,1,0:T(8,128)(2,1)S(1)}, bf16[1,72,256]{2,1,0:T(8,128)(2,1)S(1)}, u32[]{:S(2)}, u32[]{:S(2)}) collective-permute-start(bf16[1,72,256]{2,1,0:T(8,128)(2,1)S(1)} %bitcast.5), channel_id=1, source_target_pairs={{0,1},{1,0},{2,3},{3,2},{4,5},{5,4},{6,7},{7,6},{8,9},{9,8},{10,11... | collective-permute-start | bytes 110600 | tf_op jit(solution)/shard_map/ppermute | solution.py:35
  13.9 4.8 %collective-permute-start.1 = (bf16[2,72,256]{2,1,0:T(8,128)(2,1)S(1)}, bf16[2,72,256]{2,1,0:T(8,128)(2,1)S(1)}, u32[]{:S(2)}, u32[]{:S(2)}) collective-permute-start(bf16[2,72,256]{2,1,0:T(8,128)(2,1)S(1)} %join.12.a_ref), channel_id=1, source_target_pairs={{0,3},{1,2},{2,1},{3,0},{4,7},{5,6},{6,5},{7,4},{8,11},{9,10},{10,... | collective-permute-start | bytes 221192 | tf_op jit(solution)/shard_map/ppermute | solution.py:35
  16.4 9.5 %collective-permute-start.11 = (bf16[8,64,256]{2,1,0:T(8,128)(2,1)S(1)}, bf16[8,64,256]{2,1,0:T(8,128)(2,1)S(1)}, u32[]{:S(2)}, u32[]{:S(2)}) collective-permute-start(bf16[8,64,256]{2,1,0:T(8,128)(2,1)S(1)} %join.18.a_ref), channel_id=1, source_target_pairs={{0,24},{1,25},{2,26},{3,27},{4,28},{5,29},{6,30},{7,31},{8,16},{9,... | collective-permute-start | bytes 786440 | tf_op jit(solution)/shard_map/ppermute | solution.py:35
  18.7 4.4 %collective-permute-start.2 = (bf16[4,72,256]{2,1,0:T(8,128)(2,1)S(1)}, bf16[4,72,256]{2,1,0:T(8,128)(2,1)S(1)}, u32[]{:S(2)}, u32[]{:S(2)}) collective-permute-start(bf16[4,72,256]{2,1,0:T(8,128)(2,1)S(1)} %join.13.a_ref), channel_id=1, source_target_pairs={{0,32},{1,33},{2,34},{3,35},{4,36},{5,37},{6,38},{7,39},{8,40},{9,... | collective-permute-start | bytes 442376 | tf_op jit(solution)/shard_map/ppermute | solution.py:35
  23.1 11.2 %collective-permute-start.3 = (bf16[8,72,256]{2,1,0:T(8,128)(2,1)S(1)}, bf16[8,72,256]{2,1,0:T(8,128)(2,1)S(1)}, u32[]{:S(2)}, u32[]{:S(2)}) collective-permute-start(bf16[8,72,256]{2,1,0:T(8,128)(2,1)S(1)} %join.14.a_ref), channel_id=1, source_target_pairs={{0,96},{1,97},{2,98},{3,99},{4,100},{5,101},{6,102},{7,103},{8,104... | collective-permute-start | bytes 884744 | tf_op jit(solution)/shard_map/ppermute | solution.py:35
  25.9 19.7 %collective-permute-start.14 = (bf16[16,64,256]{2,1,0:T(8,128)(2,1)S(1)}, bf16[16,64,256]{2,1,0:T(8,128)(2,1)S(1)}, u32[]{:S(2)}, u32[]{:S(2)}) collective-permute-start(bf16[16,64,256]{2,1,0:T(8,128)(2,1)S(1)} %join.19.refs_5_), channel_id=1, source_target_pairs={{0,1},{1,2},{2,3},{3,0},{4,5},{5,6},{6,7},{7,4},{8,9},{9,10},{10,1... | collective-permute-start | bytes 1572872 | tf_op jit(solution)/shard_map/ppermute | solution.py:31
  26.0 2.8 %collective-permute-start.16 = (bf16[1,64,256]{2,1,0:T(8,128)(2,1)S(1)}, bf16[1,64,256]{2,1,0:T(8,128)(2,1)S(1)}, u32[]{:S(2)}, u32[]{:S(2)}) collective-permute-start(bf16[1,64,256]{2,1,0:T(8,128)(2,1)S(1)} %bitcast.7), channel_id=1, source_target_pairs={{0,8},{1,9},{2,10},{3,11},{4,12},{5,13},{6,14},{7,15},{8,0},{9,1},... | collective-permute-start | bytes 98312 | tf_op jit(solution)/shard_map/ppermute | solution.py:35
  28.8 4.3 %collective-permute-start.17 = (bf16[2,64,256]{2,1,0:T(8,128)(2,1)S(1)}, bf16[2,64,256]{2,1,0:T(8,128)(2,1)S(1)}, u32[]{:S(2)}, u32[]{:S(2)}) collective-permute-start(bf16[2,64,256]{2,1,0:T(8,128)(2,1)S(1)} %join.20.a_ref), channel_id=1, source_target_pairs={{0,24},{1,25},{2,26},{3,27},{4,28},{5,29},{6,30},{7,31},{8,16},{9,... | collective-permute-start | bytes 196616 | tf_op jit(solution)/shard_map/ppermute | solution.py:35
  33.2 4.4 %collective-permute-start.18 = (bf16[4,64,256]{2,1,0:T(8,128)(2,1)S(1)}, bf16[4,64,256]{2,1,0:T(8,128)(2,1)S(1)}, u32[]{:S(2)}, u32[]{:S(2)}) collective-permute-start(bf16[4,64,256]{2,1,0:T(8,128)(2,1)S(1)} %join.21.a_ref), channel_id=1, source_target_pairs={{0,1},{1,0},{2,3},{3,2},{4,5},{5,4},{6,7},{7,6},{8,9},{9,8},{10,11... | collective-permute-start | bytes 393224 | tf_op jit(solution)/shard_map/ppermute | solution.py:35
  34.3 14.0 %collective-permute-start.6 = (bf16[16,72,256]{2,1,0:T(8,128)(2,1)S(1)}, bf16[16,72,256]{2,1,0:T(8,128)(2,1)S(1)}, u32[]{:S(2)}, u32[]{:S(2)}) collective-permute-start(bf16[16,72,256]{2,1,0:T(8,128)(2,1)S(1)} %join.15.refs_0_), channel_id=1, source_target_pairs={{0,8},{1,9},{2,10},{3,11},{4,12},{5,13},{6,14},{7,15},{8,16},{9,17... | collective-permute-start | bytes 1769480 | tf_op jit(solution)/shard_map/ppermute | solution.py:31
  37.6 43.3 %copy-start = (bf16[8,1024,768]{2,1,0:T(8,128)(2,1)S(1)}, bf16[8,1024,768]{2,1,0:T(8,128)(2,1)}, u32[]{:S(2)}) copy-start(bf16[8,1024,768]{2,1,0:T(8,128)(2,1)} %bank_ref.3) | copy-start | bytes 37748740
  37.6 7.9 %collective-permute-start.19 = (bf16[8,64,256]{2,1,0:T(8,128)(2,1)S(1)}, bf16[8,64,256]{2,1,0:T(8,128)(2,1)S(1)}, u32[]{:S(2)}, u32[]{:S(2)}) collective-permute-start(bf16[8,64,256]{2,1,0:T(8,128)(2,1)S(1)} %join.22.a_ref), channel_id=1, source_target_pairs={{0,3},{1,2},{2,1},{3,0},{4,7},{5,6},{6,5},{7,4},{8,11},{9,10},{10,... | collective-permute-start | bytes 786440 | tf_op jit(solution)/shard_map/ppermute | solution.py:35
  41.8 9.0 %collective-permute-start.4 = (bf16[16,72,256]{2,1,0:T(8,128)(2,1)S(1)}, bf16[16,72,256]{2,1,0:T(8,128)(2,1)S(1)}, u32[]{:S(2)}, u32[]{:S(2)}) collective-permute-start(bf16[16,72,256]{2,1,0:T(8,128)(2,1)S(1)} %join.15.refs_0_), channel_id=1, source_target_pairs={{0,24},{1,25},{2,26},{3,27},{4,28},{5,29},{6,30},{7,31},{8,0},{9,1... | collective-permute-start | bytes 1769480 | tf_op jit(solution)/shard_map/ppermute | solution.py:31
  43.4 9.5 %collective-permute-start.12 = (bf16[16,64,256]{2,1,0:T(8,128)(2,1)S(1)}, bf16[16,64,256]{2,1,0:T(8,128)(2,1)S(1)}, u32[]{:S(2)}, u32[]{:S(2)}) collective-permute-start(bf16[16,64,256]{2,1,0:T(8,128)(2,1)S(1)} %join.19.refs_5_), channel_id=1, source_target_pairs={{0,3},{1,0},{2,1},{3,2},{4,7},{5,4},{6,5},{7,6},{8,11},{9,8},{10,9... | collective-permute-start | bytes 1572872 | tf_op jit(solution)/shard_map/ppermute | solution.py:31
  45.6 9.6 %collective-permute-start.22 = (bf16[16,64,256]{2,1,0:T(8,128)(2,1)S(1)}, bf16[16,64,256]{2,1,0:T(8,128)(2,1)S(1)}, u32[]{:S(2)}, u32[]{:S(2)}) collective-permute-start(bf16[16,64,256]{2,1,0:T(8,128)(2,1)S(1)} %join.23.refs_10_), channel_id=1, source_target_pairs={{0,32},{1,33},{2,34},{3,35},{4,36},{5,37},{6,38},{7,39},{8,40},{9,... | collective-permute-start | bytes 1572872 | tf_op jit(solution)/shard_map/ppermute | solution.py:31
  45.7 12.2 %collective-permute-start.20 = (bf16[16,64,256]{2,1,0:T(8,128)(2,1)S(1)}, bf16[16,64,256]{2,1,0:T(8,128)(2,1)S(1)}, u32[]{:S(2)}, u32[]{:S(2)}) collective-permute-start(bf16[16,64,256]{2,1,0:T(8,128)(2,1)S(1)} %join.23.refs_10_), channel_id=1, source_target_pairs={{0,96},{1,97},{2,98},{3,99},{4,100},{5,101},{6,102},{7,103},{8,104... | collective-permute-start | bytes 1572872 | tf_op jit(solution)/shard_map/ppermute | solution.py:31
  48.3 9.7 %collective-permute-start.15 = (bf16[8,64,256]{2,1,0:T(8,128)(2,1)S(1)}, bf16[8,64,256]{2,1,0:T(8,128)(2,1)S(1)}, u32[]{:S(2)}, u32[]{:S(2)}) collective-permute-start(bf16[8,64,256]{2,1,0:T(8,128)(2,1)S(1)} %half.9), channel_id=1, source_target_pairs={{0,1},{1,2},{2,3},{3,0},{4,5},{5,6},{6,7},{7,4},{8,9},{9,10},{10,1... | collective-permute-start | bytes 786440 | tf_op jit(solution)/shard_map/ppermute | solution.py:31
  50.8 15.7 %collective-permute-start.7 = (bf16[8,72,256]{2,1,0:T(8,128)(2,1)S(1)}, bf16[8,72,256]{2,1,0:T(8,128)(2,1)S(1)}, u32[]{:S(2)}, u32[]{:S(2)}) collective-permute-start(bf16[8,72,256]{2,1,0:T(8,128)(2,1)S(1)} %half.7), channel_id=1, source_target_pairs={{0,8},{1,9},{2,10},{3,11},{4,12},{5,13},{6,14},{7,15},{8,16},{9,17... | collective-permute-start | bytes 884744 | tf_op jit(solution)/shard_map/ppermute | solution.py:31
  52.9 13.6 %collective-permute-start.5 = (bf16[8,72,256]{2,1,0:T(8,128)(2,1)S(1)}, bf16[8,72,256]{2,1,0:T(8,128)(2,1)S(1)}, u32[]{:S(2)}, u32[]{:S(2)}) collective-permute-start(bf16[8,72,256]{2,1,0:T(8,128)(2,1)S(1)} %half.6), channel_id=1, source_target_pairs={{0,24},{1,25},{2,26},{3,27},{4,28},{5,29},{6,30},{7,31},{8,0},{9,1... | collective-permute-start | bytes 884744 | tf_op jit(solution)/shard_map/ppermute | solution.py:31
  55.2 8.3 %collective-permute-start.13 = (bf16[8,64,256]{2,1,0:T(8,128)(2,1)S(1)}, bf16[8,64,256]{2,1,0:T(8,128)(2,1)S(1)}, u32[]{:S(2)}, u32[]{:S(2)}) collective-permute-start(bf16[8,64,256]{2,1,0:T(8,128)(2,1)S(1)} %half.8), channel_id=1, source_target_pairs={{0,3},{1,0},{2,1},{3,2},{4,7},{5,4},{6,5},{7,6},{8,11},{9,8},{10,9... | collective-permute-start | bytes 786440 | tf_op jit(solution)/shard_map/ppermute | solution.py:31
  57.9 8.6 %collective-permute-start.23 = (bf16[8,64,256]{2,1,0:T(8,128)(2,1)S(1)}, bf16[8,64,256]{2,1,0:T(8,128)(2,1)S(1)}, u32[]{:S(2)}, u32[]{:S(2)}) collective-permute-start(bf16[8,64,256]{2,1,0:T(8,128)(2,1)S(1)} %half.11), channel_id=1, source_target_pairs={{0,32},{1,33},{2,34},{3,35},{4,36},{5,37},{6,38},{7,39},{8,40},{9,... | collective-permute-start | bytes 786440 | tf_op jit(solution)/shard_map/ppermute | solution.py:31
  58.0 22.9 %copy-start.1 = (s32[8,1024]{1,0:T(8,128)S(1)}, s32[8,1024]{1,0:T(8,128)}, u32[]{:S(2)}) copy-start(s32[8,1024]{1,0:T(8,128)} %labels_ref.3) | copy-start | bytes 98308
  58.0 8.5 %collective-permute-start.21 = (bf16[8,64,256]{2,1,0:T(8,128)(2,1)S(1)}, bf16[8,64,256]{2,1,0:T(8,128)(2,1)S(1)}, u32[]{:S(2)}, u32[]{:S(2)}) collective-permute-start(bf16[8,64,256]{2,1,0:T(8,128)(2,1)S(1)} %half.10), channel_id=1, source_target_pairs={{0,96},{1,97},{2,98},{3,99},{4,100},{5,101},{6,102},{7,103},{8,104... | collective-permute-start | bytes 786440 | tf_op jit(solution)/shard_map/ppermute | solution.py:31
  68.5 17.8 %collective-permute-start.24 = (bf16[8,256,768]{2,1,0:T(8,128)(2,1)S(1)}, bf16[8,256,768]{2,1,0:T(8,128)(2,1)S(1)}, u32[]{:S(2)}, u32[]{:S(2)}) collective-permute-start(bf16[8,256,768]{2,1,0:T(8,128)(2,1)S(1)} %get-tuple-element.15), channel_id=1, source_target_pairs={{0,4},{1,5},{2,6},{3,7},{4,0},{5,1},{6,2},{7,3},{8,12},{9,13},{10,... | collective-permute-start | bytes 9437192 | tf_op jit(solution)/shard_map/ppermute | solution.py:401
  92.8 29.6 %all-to-all-start = ((bf16[128,40,128]{2,1,0:T(8,128)(2,1)}), bf16[128,40,128]{2,1,0:T(8,128)(2,1)S(1)}, u32[]{:S(2)}, u32[]{:S(2)}) async-start(bf16[128,40,128]{2,1,0:T(8,128)(2,1)} %bitcast.4), calls=%async_computation | async-start | bytes 2621440 | tf_op jit(solution)/shard_map/all_to_all | solution.py:404
